TPU v7x, 256 devices: a whole 4x4x8 slice. The times are simulated.
256 devices in a mesh: context: 32 (over x, z), mirror: 2 (over core), tensor: 4 (over y).
Axes of the slice: x: 4, y: 4, z: 8, core: 2. Of those that a mesh axis runs over, the one named last changes fastest.
Arguments:
- hyena_q: bfloat16 [8192, 8192], P(('context', 'mirror'), 'tensor'), may hold values from -57 to 57
- hyena_k: bfloat16 [8192, 8192], P(('context', 'mirror'), 'tensor'), may hold values from -6 to 6
- hyena_v: bfloat16 [8192, 8192], P(('context', 'mirror'), 'tensor'), may hold values from -6 to 6
- filters: bfloat16 [512, 128], P('tensor'), may hold values from -0.5 to 0.5
- norm_gain: float32 [8192], P('tensor'), may hold values from 0.1 to 1.9
- attn_q: bfloat16 [8192, 8192], P(('context', 'mirror'), 'tensor'), may hold values from -35 to 35
- attn_k: bfloat16 [8192, 8192], P(('context', 'mirror'), 'tensor'), may hold values from -5 to 5
- out_grad: bfloat16 [8192, 8192], P(('context', 'mirror'), 'tensor'), may hold values from -20 to 20
- doc_lengths: int32 [4], replicated, may hold values from 1 to 4096, 8192 in all
Outputs:
- attn_out: bfloat16 [8192, 8192], P(('context', 'mirror'), 'tensor')
- grad_attn_q: bfloat16 [8192, 8192], P(('context', 'mirror'), 'tensor')
- grad_attn_k: bfloat16 [8192, 8192], P(('context', 'mirror'), 'tensor')
- grad_hyena_q: bfloat16 [8192, 8192], P(('context', 'mirror'), 'tensor')
- grad_hyena_k: bfloat16 [8192, 8192], P(('context', 'mirror'), 'tensor')
- grad_hyena_v: bfloat16 [8192, 8192], P(('context', 'mirror'), 'tensor')
- grad_filters: float32 [512, 128], P('tensor')
All inputs are finite; a program needn't handle non-finite values.
Results may differ from a plain program's by a relative error of at most 0.0064.
Values may be sent and summed in bfloat16 or wider, within the bound.
No kernel may reach another device: no remote copies, remote signals or barrier semaphores. Data moves between devices by JAX's collectives and lax.ppermute only.
A program may use at most 128 MiB of HBM per device.

v0:
```python
import jax
import jax.numpy as jnp
from jax import lax
from jax.sharding import PartitionSpec as P

HEAD = 128
D = 8192
REACH = 2


def passed_along(block, axis, distance):
    devices = range(lax.axis_size(axis))
    route = [(i - distance, i) for i in devices if i - distance in devices]
    return lax.ppermute(block, axis, route)


def doc_index(doc_lengths, positions):
    doc_ends = jnp.cumsum(doc_lengths, dtype=jnp.int32)
    return jnp.sum(
        (positions[:, None] >= doc_ends[None, :]).astype(jnp.int32), axis=1, dtype=jnp.int32
    )


def banded(band_table, row_count, col_count):
    repeated = jnp.tile(band_table, (1, row_count + 1))[:, : row_count * col_count]
    return repeated.reshape(band_table.shape[0], row_count, col_count)


def attend(queries, key_heads, allowed, score_scale):
    scores = (
        jnp.einsum("thd,uhd->htu", queries, key_heads, preferred_element_type=jnp.float32)
        * score_scale
    )
    row_top = jnp.max(jnp.where(allowed[None], scores, -1e30), axis=2, keepdims=True)
    row_total = jnp.sum(
        jnp.exp(jnp.where(allowed[None], scores - row_top, -1e30)), axis=2, keepdims=True
    )
    row_lse = row_top + jnp.log(row_total)
    return (jnp.where(allowed[None], jnp.exp(scores - row_lse), 0.0), row_lse)


def body(hyena_q, hyena_k, hyena_v, filters, norm_gain, attn_q, attn_k, out_grad, doc_lengths):
    tok_rows, channels = hyena_q.shape
    groups, tap_count = filters.shape
    group_width = channels // groups
    heads_dev = channels // HEAD
    pad_rows = tok_rows + tap_count
    offset = lax.axis_index(("context", "mirror")) * tok_rows
    score_scale = HEAD ** (-0.5)
    window_span = REACH * tok_rows
    own_pos = offset + jnp.arange(tok_rows, dtype=jnp.int32)
    own_doc = doc_index(doc_lengths, own_pos)
    kv_product = (hyena_k.astype(jnp.float32) * hyena_v.astype(jnp.float32)).astype(jnp.bfloat16)
    left_rim = passed_along(kv_product[tok_rows - (tap_count - 1) :], ("context", "mirror"), 1)
    wide_pad = jnp.concatenate(
        [left_rim, kv_product, jnp.zeros((1, channels), jnp.bfloat16)], axis=0
    )
    wide_pos = offset - (tap_count - 1) + jnp.arange(pad_rows, dtype=jnp.int32)
    fwd_mask = own_doc[:, None] == doc_index(doc_lengths, wide_pos)[None, :]
    zeros_tail = jnp.zeros((groups, pad_rows + 1 - tap_count), jnp.bfloat16)
    fwd_table = jnp.concatenate([filters[:, ::-1], zeros_tail], axis=1)
    fwd_band = banded(fwd_table, tok_rows, pad_rows) * fwd_mask[None].astype(jnp.bfloat16)
    wide_groups = wide_pad.reshape(pad_rows, groups, group_width)
    signal = jnp.einsum(
        "gtu,ugc->tgc", fwd_band, wide_groups, preferred_element_type=jnp.float32
    ).reshape(tok_rows, channels)
    hyena_mix = hyena_q.astype(jnp.float32) * signal
    square_sum = lax.psum(jnp.sum(hyena_mix * hyena_mix, axis=1), "tensor")
    inv_rms = lax.rsqrt(square_sum / D + 1e-06)
    values = (hyena_mix * inv_rms[:, None] * norm_gain[None, :]).astype(jnp.bfloat16)
    earlier = []
    for distance in range(1, REACH + 1):
        earlier.append(passed_along((attn_k, values), ("context", "mirror"), distance))
    key_win = jnp.concatenate([piece[0] for piece in earlier[::-1]] + [attn_k], axis=0)
    value_win = jnp.concatenate([piece[1] for piece in earlier[::-1]] + [values], axis=0)
    window = (REACH + 1) * tok_rows
    key_pos = offset - REACH * tok_rows + jnp.arange(window, dtype=jnp.int32)
    key_doc = doc_index(doc_lengths, key_pos)
    allowed = (
        (key_pos[None, :] >= 0)
        & (key_pos[None, :] <= own_pos[:, None])
        & (own_pos[:, None] - key_pos[None, :] <= window_span)
        & (key_doc[None, :] == own_doc[:, None])
    )
    queries = attn_q.reshape(tok_rows, heads_dev, HEAD)
    grad_heads = out_grad.reshape(tok_rows, heads_dev, HEAD)
    key_heads = key_win.reshape(window, heads_dev, HEAD)
    value_heads = value_win.reshape(window, heads_dev, HEAD)
    attn_prob, row_lse = attend(queries, key_heads, allowed, score_scale)
    prob_half = attn_prob.astype(jnp.bfloat16)
    attn_out = (
        jnp.einsum("htu,uhd->thd", prob_half, value_heads, preferred_element_type=jnp.float32)
        .astype(jnp.bfloat16)
        .reshape(tok_rows, channels)
    )
    grad_prob = jnp.einsum(
        "thd,uhd->htu", grad_heads, value_heads, preferred_element_type=jnp.float32
    )
    row_delta = jnp.sum(attn_prob * grad_prob, axis=2, keepdims=True)
    grad_score = (attn_prob * (grad_prob - row_delta) * score_scale).astype(jnp.bfloat16)
    grad_attn_q = (
        jnp.einsum("htu,uhd->thd", grad_score, key_heads, preferred_element_type=jnp.float32)
        .astype(jnp.bfloat16)
        .reshape(tok_rows, channels)
    )
    own_start = REACH * tok_rows
    key_part = jnp.einsum("htu,thd->uhd", grad_score, queries, preferred_element_type=jnp.float32)
    value_part = jnp.einsum(
        "htu,thd->uhd", prob_half, grad_heads, preferred_element_type=jnp.float32
    )
    grad_keys = key_part[own_start:]
    grad_vals = value_part[own_start:]
    for distance in range(1, REACH + 1):
        low_row = (REACH - distance) * tok_rows
        returned = passed_along(
            (key_part[low_row : low_row + tok_rows], value_part[low_row : low_row + tok_rows]),
            ("context", "mirror"),
            -distance,
        )
        grad_keys = grad_keys + returned[0]
        grad_vals = grad_vals + returned[1]
    grad_attn_k = grad_keys.astype(jnp.bfloat16).reshape(tok_rows, channels)
    grad_values = grad_vals.reshape(tok_rows, channels)
    inner_sum = lax.psum(jnp.sum(norm_gain[None, :] * grad_values * hyena_mix, axis=1), "tensor")
    grad_mix = inv_rms[:, None] * (
        norm_gain[None, :] * grad_values - hyena_mix * (inner_sum * inv_rms * inv_rms / D)[:, None]
    )
    grad_hyena_q = (grad_mix * signal).astype(jnp.bfloat16)
    grad_signal = (grad_mix * hyena_q.astype(jnp.float32)).astype(jnp.bfloat16)
    right_rim = passed_along(grad_signal[: tap_count - 1], ("context", "mirror"), -1)
    back_pad = jnp.concatenate(
        [grad_signal, right_rim, jnp.zeros((1, channels), jnp.bfloat16)], axis=0
    )
    back_pos = offset + jnp.arange(pad_rows, dtype=jnp.int32)
    back_mask = own_doc[:, None] == doc_index(doc_lengths, back_pos)[None, :]
    back_table = jnp.concatenate([filters, zeros_tail], axis=1)
    back_band = banded(back_table, tok_rows, pad_rows) * back_mask[None].astype(jnp.bfloat16)
    grad_kv = jnp.einsum(
        "gtu,ugc->tgc",
        back_band,
        back_pad.reshape(pad_rows, groups, group_width),
        preferred_element_type=jnp.float32,
    ).reshape(tok_rows, channels)
    grad_hyena_k = (grad_kv * hyena_v.astype(jnp.float32)).astype(jnp.bfloat16)
    grad_hyena_v = (grad_kv * hyena_k.astype(jnp.float32)).astype(jnp.bfloat16)
    block_count = 4
    block_size = groups // block_count
    mask_float = fwd_mask.astype(jnp.float32)

    def filter_block(pieces):
        grad_block, wide_block = pieces
        correlation = (
            jnp.einsum("tgc,ugc->gtu", grad_block, wide_block, preferred_element_type=jnp.float32)
            * mask_float[None]
        )
        flattened = jnp.pad(
            correlation.reshape(block_size, tok_rows * pad_rows), ((0, 0), (0, tok_rows))
        )
        diagonal = flattened.reshape(block_size, tok_rows, pad_rows + 1)[:, :, :tap_count]
        return jnp.sum(diagonal, axis=1)[:, ::-1]

    grad_blocks = grad_signal.reshape(tok_rows, block_count, block_size, group_width).transpose(
        1, 0, 2, 3
    )
    wide_blocks = wide_groups.reshape(pad_rows, block_count, block_size, group_width).transpose(
        1, 0, 2, 3
    )
    local_filters = lax.map(filter_block, (grad_blocks, wide_blocks)).reshape(groups, tap_count)
    grad_filters = lax.psum(local_filters, ("context", "mirror"))
    return (
        attn_out,
        grad_attn_q,
        grad_attn_k,
        grad_hyena_q,
        grad_hyena_k,
        grad_hyena_v,
        grad_filters,
    )


def solution(mesh):
    return jax.shard_map(
        body,
        mesh=mesh,
        in_specs=(
            P(("context", "mirror"), "tensor"),
            P(("context", "mirror"), "tensor"),
            P(("context", "mirror"), "tensor"),
            P("tensor", None),
            P("tensor"),
            P(("context", "mirror"), "tensor"),
            P(("context", "mirror"), "tensor"),
            P(("context", "mirror"), "tensor"),
            P(),
        ),
        out_specs=(
            P(("context", "mirror"), "tensor"),
            P(("context", "mirror"), "tensor"),
            P(("context", "mirror"), "tensor"),
            P(("context", "mirror"), "tensor"),
            P(("context", "mirror"), "tensor"),
            P(("context", "mirror"), "tensor"),
            P("tensor", None),
        ),
        check_vma=False,
    )
```

profile of v0, /device:TPU:1, one launch (start us, length us, event | category | flops | bytes accessed | tf_op | source)
XLA Modules:
  0.0 418.3 jit_solution(6076285192775258305)
XLA Ops:
  8.6 5.1 %collective-permute-start.4 = (bf16[128,2048]{0,1:T(8,128)(2,1)S(1)}, bf16[128,2048]{0,1:T(8,128)(2,1)}, u32[]{:S(2)}, u32[]{:S(2)}) collective-permute-start(bf16[128,2048]{0,1:T(8,128)(2,1)S(1)} %copy.70), channel_id=1, source_target_pairs={{0,4},{4,8},{8,12},{12,16},{16,20},{20,24},{24,28},{28,32},{32,36}... | collective-permute-start | bytes 1572872 | tf_op jit(solution)/shard_map/ppermute | solution.py:14
  13.7 4.4 %collective-permute-start.3 = (bf16[128,2048]{0,1:T(8,128)(2,1)S(1)}, bf16[128,2048]{0,1:T(8,128)(2,1)}, u32[]{:S(2)}, u32[]{:S(2)}) collective-permute-start(bf16[128,2048]{0,1:T(8,128)(2,1)S(1)} %copy.70), channel_id=1, source_target_pairs={{0,8},{4,12},{8,16},{12,20},{16,24},{20,28},{24,32},{28,36},{32,40... | collective-permute-start | bytes 1572872 | tf_op jit(solution)/shard_map/ppermute | solution.py:14
  19.4 1.5 copy.66
  22.9 1.9 collective-permute-start
  28.5 4.5 %tile.8 = bf16[128,129,257]{0,2,1:T(8,128)(2,1)} broadcast(bf16[128,257]{0,1:T(8,128)(2,1)S(1)} %concatenate.19.clone), dimensions={0,2} | broadcast | bytes 8552960 | tf_op jit(solution)/shard_map/tile | solution.py:25
  33.0 13.2 %tile.9 = bf16[128,33153]{0,1:T(8,128)(2,1)} reshape(bf16[128,129,257]{0,2,1:T(8,128)(2,1)} %tile.8) | data formatting | bytes 16974336 | tf_op jit(solution)/shard_map/tile | solution.py:25
  46.3 7.1 %slice.49 = bf16[128,32768]{0,1:T(8,128)(2,1)} slice(bf16[128,33153]{0,1:T(8,128)(2,1)} %tile.9), slice={[0:128], [0:32768]} | slice | bytes 16777216 | tf_op jit(solution)/shard_map/slice | solution.py:25
  53.3 12.5 %copy.69 = bf16[128,128,256]{2,1,0:T(8,128)(2,1)} copy(bf16[128,128,256]{0,2,1:T(8,128)(2,1)} %bitcast.165) | data formatting | bytes 16777216 | tf_op jit(solution)/shard_map/reshape | solution.py:26
  65.8 4.5 %tile.20 = bf16[128,129,257]{0,2,1:T(8,128)(2,1)} broadcast(bf16[128,257]{0,1:T(8,128)(2,1)S(1)} %concatenate.23.clone), dimensions={0,2} | broadcast | bytes 8552960 | tf_op jit(solution)/shard_map/tile | solution.py:25
  70.3 13.2 %tile.21 = bf16[128,33153]{0,1:T(8,128)(2,1)} reshape(bf16[128,129,257]{0,2,1:T(8,128)(2,1)} %tile.20) | data formatting | bytes 16974336 | tf_op jit(solution)/shard_map/tile | solution.py:25
  83.5 7.1 %slice.57 = bf16[128,32768]{0,1:T(8,128)(2,1)} slice(bf16[128,33153]{0,1:T(8,128)(2,1)} %tile.21), slice={[0:128], [0:32768]} | slice | bytes 16777216 | tf_op jit(solution)/shard_map/slice | solution.py:25
  90.6 12.6 %copy.84 = bf16[128,128,256]{2,1,0:T(8,128)(2,1)} copy(bf16[128,128,256]{0,2,1:T(8,128)(2,1)} %bitcast.166) | data formatting | bytes 16777216 | tf_op jit(solution)/shard_map/reshape | solution.py:26
  103.7 1.4 pad_maximum_fusion.1
  107.7 1.6 collective-permute-start.8
  109.3 3.4 collective-permute-start.7
  112.7 1.5 maximum_maximum_fusion
  114.2 2.3 fusion.10
  116.6 16.7 %collective-permute-done.8 = f32[128,16,128]{0,2,1:T(8,128)S(1)} collective-permute-done((f32[128,16,128]{0,2,1:T(8,128)S(1)}, f32[128,16,128]{0,2,1:T(8,128)S(1)}, u32[]{:S(2)}, u32[]{:S(2)}) %collective-permute-start.8) | collective-permute-done | bytes 1048608 | tf_op jit(solution)/shard_map/ppermute | solution.py:14
  133.3 12.7 %collective-permute-done.7 = f32[128,16,128]{0,2,1:T(8,128)S(1)} collective-permute-done((f32[128,16,128]{0,2,1:T(8,128)S(1)}, f32[128,16,128]{0,2,1:T(8,128)S(1)}, u32[]{:S(2)}, u32[]{:S(2)}) %collective-permute-start.7) | collective-permute-done | bytes 1048608 | tf_op jit(solution)/shard_map/ppermute | solution.py:14
  147.2 8.7 %all-reduce.3 = (f32[128]{0:T(128)S(1)}, f32[128]{0:T(128)S(1)}) all-reduce(f32[128]{0:T(128)S(1)} %get-tuple-element.111, f32[128]{0:T(128)S(1)} %get-tuple-element.110), channel_id=1, replica_groups=mesh['context'=32,'mirror'=2,'tensor'=4] {'tensor'}, use_global_device_ids=true, to_apply=%region_4.5 | all-reduce | flops 256 | bytes 2048 | tf_op jit(solution)/shard_map/psum | solution.py:68
  155.9 3.4 fusion.45
  159.2 3.8 collective-permute-start.2
  163.0 5.2 %collective-permute-start.1 = (bf16[128,2048]{0,1:T(8,128)(2,1)}, bf16[128,2048]{0,1:T(8,128)(2,1)}, u32[]{:S(2)}, u32[]{:S(2)}) collective-permute-start(bf16[128,2048]{0,1:T(8,128)(2,1)} %get-tuple-element.134), channel_id=1, source_target_pairs={{0,8},{4,12},{8,16},{12,20},{16,24},{20,28},{24,32},{28,36},{32,40... | collective-permute-start | bytes 1572872 | tf_op jit(solution)/shard_map/ppermute | solution.py:14
  168.2 1.9 collective-permute-start.9
  170.1 67.7 %while.13 = (s32[]{:T(128)}, f32[4,32,128]{2,1,0:T(8,128)}, bf16[4,128,32,16]{1,3,2,0:T(8,128)(2,1)}, bf16[4,256,32,16]{1,3,2,0:T(8,128)(2,1)}, s32[256]{0:T(256...) while((s32[]{:T(128)}, f32[4,32,128]{2,1,0:T(8,128)}, bf16[4,128,32,16]{1,3,2,0:T(8,128)(2,1)}, ...), condition=%wide.region_14.15_spmd.clone, body=%wide.region_12.14_spmd.clone.sunk | while | flops 35188736 | bytes 32246372 | solution.py:168
  170.2 1.8 convolution_multiply_fusion.2
  172.0 2.4 copy.103
  174.5 2.2 pad.33
  176.7 8.0 %reshape.319 = f32[32,128,257]{2,1,0:T(8,128)} reshape(f32[32,32896]{1,0:T(8,128)} %pad.33) | data formatting | bytes 8421376 | tf_op jit(solution)/shard_map/while/body/eval_jaxpr/reshape | solution.py:159
  184.7 1.7 slice_reduce_fusion.2
  187.2 1.8 convolution_multiply_fusion.2
  188.9 2.4 copy.103
  191.4 2.2 pad.33
  193.6 8.0 %reshape.319 = f32[32,128,257]{2,1,0:T(8,128)} reshape(f32[32,32896]{1,0:T(8,128)} %pad.33) | data formatting | bytes 8421376 | tf_op jit(solution)/shard_map/while/body/eval_jaxpr/reshape | solution.py:159
  201.6 1.7 slice_reduce_fusion.2
  204.1 1.8 convolution_multiply_fusion.2
  205.9 2.4 copy.103
  208.3 2.2 pad.33
  210.6 8.0 %reshape.319 = f32[32,128,257]{2,1,0:T(8,128)} reshape(f32[32,32896]{1,0:T(8,128)} %pad.33) | data formatting | bytes 8421376 | tf_op jit(solution)/shard_map/while/body/eval_jaxpr/reshape | solution.py:159
  218.5 1.7 slice_reduce_fusion.2
  221.0 1.8 convolution_multiply_fusion.2
  222.8 2.4 copy.103
  225.2 2.2 pad.33
  227.5 8.0 %reshape.319 = f32[32,128,257]{2,1,0:T(8,128)} reshape(f32[32,32896]{1,0:T(8,128)} %pad.33) | data formatting | bytes 8421376 | tf_op jit(solution)/shard_map/while/body/eval_jaxpr/reshape | solution.py:159
  235.4 1.7 slice_reduce_fusion.2
  237.8 2.0 copy.88
  239.9 1.4 maximum_maximum_fusion.1
  241.4 6.7 %fusion.8 = f32[128,16,128]{2,1,0:T(8,128)} fusion(bf16[256,128,16]{0,2,1:T(8,128)(2,1)S(1)} %bitcast.175, bf16[128,128,256]{2,1,0:T(8,128)(2,1)} %copy.84, bf16[128,256]{1,0:T(8,128)(2,1)S(1)} %get-tuple-element.137), kind=kOutput, calls=%fused_computation.11 | convolution fusion | flops 138412032 | bytes 10551296 | tf_op jit(solution)/shard_map/gtu,ugc->tgc/dot_general | solution.py:138
  248.1 1.6 pad_maximum_fusion
  250.9 2.3 fusion.72
  253.2 6.6 %convolution_bitcast_fusion.1 = f32[384,16,128]{0,2,1:T(8,128)} fusion(bf16[128,16,128]{0,2,1:T(8,128)(2,1)} %bitcast.177, f32[16,384,128]{2,1,0:T(8,128)} %fusion.72, f32[16,384,128]{2,1,0:T(8,128)S(1)} %get-tuple-element.142, f32[16,128]{1,0:T(8,128)S(1)} %log_add_fusion, pred[128,384]{0,1:T(8,128)(4,1)S(1)} %fusion.54), kind=kOutput, calls=%fused_computation.32 | convolution fusion | flops 209979776 | bytes 10018816 | tf_op jit(solution)/shard_map/htu,thd->uhd/dot_general | solution.py:107
  259.8 3.4 fusion.70
  264.5 2.1 collective-permute-start.5
  267.8 2.0 copy.89
  269.9 2.0 copy.90
  271.9 3.0 convolution_convert_fusion
  274.9 2.0 copy.85
  276.9 6.2 %fusion.44 = bf16[16,128,128]{2,1,0:T(8,128)(2,1)} fusion(bf16[384,16,128]{0,2,1:T(8,128)(2,1)} %bitcast.172, f32[16,384,128]{2,1,0:T(8,128)} %fusion.72, f32[16,384,128]{2,1,0:T(8,128)S(1)} %get-tuple-element.142, f32[16,128]{1,0:T(8,128)S(1)} %log_add_fusion, pred[128,384]{0,1:T(8,128)(4,1)S(1)} %fusion.54), kind=kOutput, calls=%fused_computation.54 | convolution fusion | flops 210241920 | bytes 8445952 | tf_op jit(solution)/shard_map/htu,uhd->thd/dot_general | solution.py:102
  283.1 2.0 copy.86
  285.2 5.1 %collective-permute-done.6 = f32[128,16,128]{0,2,1:T(8,128)} collective-permute-done((f32[128,16,128]{0,2,1:T(8,128)}, f32[128,16,128]{0,2,1:T(8,128)}, u32[]{:S(2)}, u32[]{:S(2)}) %collective-permute-start.6) | collective-permute-done | bytes 1048608 | tf_op jit(solution)/shard_map/ppermute | solution.py:14
  290.3 11.6 %collective-permute-done.5 = f32[128,16,128]{0,2,1:T(8,128)} collective-permute-done((f32[128,16,128]{0,2,1:T(8,128)}, f32[128,16,128]{0,2,1:T(8,128)}, u32[]{:S(2)}, u32[]{:S(2)}) %collective-permute-start.5) | collective-permute-done | bytes 1048608 | tf_op jit(solution)/shard_map/ppermute | solution.py:14
  301.8 2.0 fusion.51
  304.9 105.0 %all-reduce.6.cloned.1.call-done = f32[128,128]{1,0:T(8,128)} async-done(((f32[128,128]{1,0:T(8,128)}), f32[128,128]{1,0:T(8,128)}) %all-reduce.6.cloned.1.call-update) | async-done | bytes 65552 | tf_op jit(solution)/shard_map/psum | solution.py:169
  410.0 1.5 copy.114
  (104 shorter events, 20.3 us)
Async XLA Ops:
  7.2 17.6 %copy-start.19 = (bf16[128,128]{1,0:T(8,128)(2,1)S(1)}, bf16[128,128]{1,0:T(8,128)(2,1)}, u32[]{:S(2)}) copy-start(bf16[128,128]{1,0:T(8,128)(2,1)} %param.14) | copy-start | bytes 98308
  7.2 17.9 %copy-start.16 = (bf16[128,2048]{1,0:T(8,128)(2,1)S(1)}, bf16[128,2048]{1,0:T(8,128)(2,1)}, u32[]{:S(2)}) copy-start(bf16[128,2048]{1,0:T(8,128)(2,1)} %param.11) | copy-start | bytes 1572868
  7.2 402.8 %all-reduce.6.cloned.1.call-start = ((), (), s32[]{:S(2)}) async-start(), calls=%async_computation | async-start | bytes 131072 | tf_op jit(solution)/shard_map/psum | solution.py:169
  8.6 17.4 %copy-start.17 = (bf16[128,2048]{1,0:T(8,128)(2,1)S(1)}, bf16[128,2048]{1,0:T(8,128)(2,1)}, u32[]{:S(2)}) copy-start(bf16[128,2048]{1,0:T(8,128)(2,1)} %param.18) | copy-start | bytes 1572868
  8.6 95.0 %collective-permute-start.4 = (bf16[128,2048]{0,1:T(8,128)(2,1)S(1)}, bf16[128,2048]{0,1:T(8,128)(2,1)}, u32[]{:S(2)}, u32[]{:S(2)}) collective-permute-start(bf16[128,2048]{0,1:T(8,128)(2,1)S(1)} %copy.70), channel_id=1, source_target_pairs={{0,4},{4,8},{8,12},{12,16},{16,20},{20,24},{24,28},{28,32},{32,36}... | collective-permute-start | bytes 1572872 | tf_op jit(solution)/shard_map/ppermute | solution.py:14
  13.7 90.0 %collective-permute-start.3 = (bf16[128,2048]{0,1:T(8,128)(2,1)S(1)}, bf16[128,2048]{0,1:T(8,128)(2,1)}, u32[]{:S(2)}, u32[]{:S(2)}) collective-permute-start(bf16[128,2048]{0,1:T(8,128)(2,1)S(1)} %copy.70), channel_id=1, source_target_pairs={{0,8},{4,12},{8,16},{12,20},{16,24},{20,28},{24,32},{28,36},{32,40... | collective-permute-start | bytes 1572872 | tf_op jit(solution)/shard_map/ppermute | solution.py:14
  19.3 9.1 %copy-start.8 = (bf16[128,2048]{0,1:T(8,128)(2,1)}, bf16[128,2048]{0,1:T(8,128)(2,1)S(1)}, u32[]{:S(2)}) copy-start(bf16[128,2048]{0,1:T(8,128)(2,1)S(1)} %copy.67) | copy-start | bytes 1572868
  19.4 7.7 %copy-start.21 = (s32[4]{0:T(128)S(1)}, s32[4]{0:T(128)}, u32[]{:S(2)}) copy-start(s32[4]{0:T(128)} %param.19) | copy-start | bytes 52
  19.4 8.0 %copy-start.18 = (bf16[128,2048]{1,0:T(8,128)(2,1)S(1)}, bf16[128,2048]{1,0:T(8,128)(2,1)}, u32[]{:S(2)}) copy-start(bf16[128,2048]{1,0:T(8,128)(2,1)} %param.16) | copy-start | bytes 1572868
  20.9 12.1 %copy-start.10 = (bf16[128,2048]{0,1:T(8,128)(2,1)}, bf16[128,2048]{0,1:T(8,128)(2,1)S(1)}, u32[]{:S(2)}) copy-start(bf16[128,2048]{0,1:T(8,128)(2,1)S(1)} %copy.66) | copy-start | bytes 1572868
  21.1 0.8 copy-start.6
  22.9 89.8 %collective-permute-start = (bf16[127,2048]{0,1:T(8,128)(2,1)}, bf16[127,2048]{0,1:T(8,128)(2,1)}, u32[]{:S(2)}, u32[]{:S(2)}) collective-permute-start(bf16[127,2048]{0,1:T(8,128)(2,1)} %slice.48), channel_id=1, source_target_pairs={{0,4},{4,8},{8,12},{12,16},{16,20},{20,24},{24,28},{28,32},{32,36}... | collective-permute-start | bytes 1560584 | tf_op jit(solution)/shard_map/ppermute | solution.py:14
  103.1 1.9 copy-start.15
  105.1 1.5 copy-start.4
  105.1 1.5 copy-start.12
  105.9 8.3 %slice-start = ((s8[8388608]{0:T(1024)(128)(4,1)}), s8[4194304]{0:T(1024)(128)(4,1)S(1)}, s32[]{:S(2)}) async-start(s8[8388608]{0:T(1024)(128)(4,1)} %bitcast.163), calls=%async_computation.1 | async-start | bytes 8388608
  106.6 7.6 %slice-start.1 = ((s8[8388608]{0:T(1024)(128)(4,1)}), s8[4194304]{0:T(1024)(128)(4,1)S(1)}, s32[]{:S(2)}) async-start(s8[8388608]{0:T(1024)(128)(4,1)} %bitcast.163), calls=%async_computation.2 | async-start | bytes 8388608
  107.4 5.2 %copy-start.7 = (bf16[128,2048]{0,1:T(8,128)(2,1)S(1)}, bf16[128,2048]{0,1:T(8,128)(2,1)}, u32[]{:S(2)}) copy-start(bf16[128,2048]{0,1:T(8,128)(2,1)} %copy-done.6) | copy-start | bytes 1572868
  107.7 25.6 %collective-permute-start.8 = (f32[128,16,128]{0,2,1:T(8,128)S(1)}, f32[128,16,128]{0,2,1:T(8,128)S(1)}, u32[]{:S(2)}, u32[]{:S(2)}) collective-permute-start(f32[128,16,128]{0,2,1:T(8,128)S(1)} %get-tuple-element.131), channel_id=1, source_target_pairs={{8,0},{12,4},{16,8},{20,12},{24,16},{28,20},{32,24},{36,28},{40,32... | collective-permute-start | bytes 3145736 | tf_op jit(solution)/shard_map/ppermute | solution.py:14
  109.3 36.7 %collective-permute-start.7 = (f32[128,16,128]{0,2,1:T(8,128)S(1)}, f32[128,16,128]{0,2,1:T(8,128)S(1)}, u32[]{:S(2)}, u32[]{:S(2)}) collective-permute-start(f32[128,16,128]{0,2,1:T(8,128)S(1)} %get-tuple-element.130), channel_id=1, source_target_pairs={{4,0},{8,4},{12,8},{16,12},{20,16},{24,20},{28,24},{32,28},{36,32}... | collective-permute-start | bytes 3145736 | tf_op jit(solution)/shard_map/ppermute | solution.py:14
  114.2 2.3 copy-start
  116.5 30.0 %copy-start.1 = (f32[128,16,128]{2,1,0:T(8,128)}, f32[128,16,128]{2,1,0:T(8,128)S(1)}, u32[]{:S(2)}) copy-start(f32[128,16,128]{2,1,0:T(8,128)S(1)} %fusion.10) | copy-start | bytes 3145732
  116.5 29.7 %copy-start.5 = (bf16[128,2048]{0,1:T(8,128)(2,1)S(1)}, bf16[128,2048]{0,1:T(8,128)(2,1)}, u32[]{:S(2)}) copy-start(bf16[128,2048]{0,1:T(8,128)(2,1)} %copy.65) | copy-start | bytes 1572868
  116.5 29.6 %copy-start.20 = (f32[2048]{0:T(1024)S(1)}, f32[2048]{0:T(1024)}, u32[]{:S(2)}) copy-start(f32[2048]{0:T(1024)} %param.15) | copy-start | bytes 24580
  146.2 1.0 copy-start.2
  159.2 88.9 %collective-permute-start.2 = (bf16[128,2048]{0,1:T(8,128)(2,1)}, bf16[128,2048]{0,1:T(8,128)(2,1)}, u32[]{:S(2)}, u32[]{:S(2)}) collective-permute-start(bf16[128,2048]{0,1:T(8,128)(2,1)} %get-tuple-element.134), channel_id=1, source_target_pairs={{0,4},{4,8},{8,12},{12,16},{16,20},{20,24},{24,28},{28,32},{32,36}... | collective-permute-start | bytes 1572872 | tf_op jit(solution)/shard_map/ppermute | solution.py:14
  163.0 85.1 %collective-permute-start.1 = (bf16[128,2048]{0,1:T(8,128)(2,1)}, bf16[128,2048]{0,1:T(8,128)(2,1)}, u32[]{:S(2)}, u32[]{:S(2)}) collective-permute-start(bf16[128,2048]{0,1:T(8,128)(2,1)} %get-tuple-element.134), channel_id=1, source_target_pairs={{0,8},{4,12},{8,16},{12,20},{16,24},{20,28},{24,32},{28,36},{32,40... | collective-permute-start | bytes 1572872 | tf_op jit(solution)/shard_map/ppermute | solution.py:14
  168.2 71.7 %collective-permute-start.9 = (bf16[127,2048]{0,1:T(8,128)(2,1)}, bf16[127,2048]{0,1:T(8,128)(2,1)}, u32[]{:S(2)}, u32[]{:S(2)}) collective-permute-start(bf16[127,2048]{0,1:T(8,128)(2,1)} %bitcast.150), channel_id=1, source_target_pairs={{4,0},{8,4},{12,8},{16,12},{20,16},{24,20},{28,24},{32,28},{36,32}... | collective-permute-start | bytes 1560584 | tf_op jit(solution)/shard_map/ppermute | solution.py:14
  248.1 2.8 copy-start.13
  249.7 1.2 copy-start.3
  259.8 6.8 %copy-start.9 = (bf16[128,2048]{0,1:T(8,128)(2,1)S(1)}, bf16[128,2048]{0,1:T(8,128)(2,1)}, u32[]{:S(2)}) copy-start(bf16[128,2048]{0,1:T(8,128)(2,1)} %copy-done.8) | copy-start | bytes 1572868
  259.8 6.8 %copy-start.11 = (bf16[128,2048]{0,1:T(8,128)(2,1)S(1)}, bf16[128,2048]{0,1:T(8,128)(2,1)}, u32[]{:S(2)}) copy-start(bf16[128,2048]{0,1:T(8,128)(2,1)} %copy-done.10) | copy-start | bytes 1572868
  259.8 6.8 %copy-start.14 = (f32[128,16,128]{2,1,0:T(8,128)S(1)}, f32[128,16,128]{2,1,0:T(8,128)}, u32[]{:S(2)}) copy-start(f32[128,16,128]{2,1,0:T(8,128)} %fusion.8) | copy-start | bytes 3145732
  263.2 27.1 %collective-permute-start.6 = (f32[128,16,128]{0,2,1:T(8,128)}, f32[128,16,128]{0,2,1:T(8,128)}, u32[]{:S(2)}, u32[]{:S(2)}) collective-permute-start(f32[128,16,128]{0,2,1:T(8,128)} %get-tuple-element.129), channel_id=1, source_target_pairs={{8,0},{12,4},{16,8},{20,12},{24,16},{28,20},{32,24},{36,28},{40,32... | collective-permute-start | bytes 3145736 | tf_op jit(solution)/shard_map/ppermute | solution.py:14
  264.5 37.4 %collective-permute-start.5 = (f32[128,16,128]{0,2,1:T(8,128)}, f32[128,16,128]{0,2,1:T(8,128)}, u32[]{:S(2)}, u32[]{:S(2)}) collective-permute-start(f32[128,16,128]{0,2,1:T(8,128)} %get-tuple-element.128), channel_id=1, source_target_pairs={{4,0},{8,4},{12,8},{16,12},{20,16},{24,20},{28,24},{32,28},{36,32}... | collective-permute-start | bytes 3145736 | tf_op jit(solution)/shard_map/ppermute | solution.py:14
Sparse Core Ops, SparseCore 0:
  240.0 169.8 all-reduce.5
where the time goes:
time: 421 us; the launch traced here: 418 us
  local copies, waits for them, and re-layouts  155 us (37%)
  waiting for transfers between devices  151 us (36%)
  matrix products  35.9 us (9%)
  starting transfers between devices  30.6 us (7%)
  other arithmetic  21.9 us (5%)
  between operations  14.5 us (3%)
  blocking collectives  8.7 us (2%)
    psum x1, waiting for transfers between devices, body(): grad_filters = lax.psum(local_filters, ('context', 'mirror'))  105 us
    ppermute x10, waiting for transfers between devices, passed_along(): return lax.ppermute(block, axis, route)  46.1 us
    another operation x4, local copies, waits for them, and re-layouts, banded(): jnp.tile(band_table, (1, row_count + 1))[:, :row_count * col_count]  35.4 us
    reshape x4, local copies, waits for them, and re-layouts, filter_block(): flattened.reshape(block_size, tok_rows, pad_rows + 1)[:, :, :tap_count]  31.8 us
    ppermute x10, starting transfers between devices, passed_along(): return lax.ppermute(block, axis, route)  30.6 us
    reshape x2, local copies, waits for them, and re-layouts, banded(): return repeated.reshape(band_table.shape[0], row_count, col_count)  25 us
    unnamed x61, local copies, waits for them, and re-layouts  20.7 us
    slice x2, local copies, waits for them, and re-layouts, banded(): jnp.tile(band_table, (1, row_count + 1))[:, :row_count * col_count]  14.1 us
  transfers between devices with their start and end apart: 11, of which 5 were waited for; matrix products, arithmetic and copies ran while one was open for 49% of the time, Pallas kernels for 0%

commit v1 on v0

--- a/solution.py
+++ b/solution.py
@@ -6,6 +6,12 @@
 HEAD = 128
 D = 8192
 REACH = 2
+
+
+def add_all(x, name):
+    blocks = lax.all_gather(x, name, axis=0, tiled=False)
+    acc = blocks.sum(axis=0)
+    return acc
 
 
 def passed_along(block, axis, distance):
@@ -166,7 +172,7 @@
         1, 0, 2, 3
     )
     local_filters = lax.map(filter_block, (grad_blocks, wide_blocks)).reshape(groups, tap_count)
-    grad_filters = lax.psum(local_filters, ("context", "mirror"))
+    grad_filters = add_all(local_filters, ("context", "mirror"))
     return (
         attn_out,
         grad_attn_q,

time: 421 us -> 330 us (0.78)
  the two profiles are of different devices: /device:TPU:1 before, /device:TPU:3 now
where the time goes in v1:
time: 330 us; the launch traced here: 327 us
  local copies, waits for them, and re-layouts  154 us (47%)
  waiting for transfers between devices  57.8 us (18%)
  matrix products  36 us (11%)
  starting transfers between devices  31 us (9%)
  other arithmetic  24.7 us (7%)
  between operations  14.6 us (4%)
  blocking collectives  8.88 us (3%)
    ppermute x10, waiting for transfers between devices, passed_along(): return lax.ppermute(block, axis, route)  57.7 us
    another operation x4, local copies, waits for them, and re-layouts, banded(): jnp.tile(band_table, (1, row_count + 1))[:, :row_count * col_count]  35.3 us
    reshape x4, local copies, waits for them, and re-layouts, filter_block(): flattened.reshape(block_size, tok_rows, pad_rows + 1)[:, :, :tap_count]  32 us
    ppermute x10, starting transfers between devices, passed_along(): return lax.ppermute(block, axis, route)  31 us
    reshape x2, local copies, waits for them, and re-layouts, banded(): return repeated.reshape(band_table.shape[0], row_count, col_count)  24.8 us
    unnamed x62, local copies, waits for them, and re-layouts  19.3 us
    slice x2, local copies, waits for them, and re-layouts, banded(): jnp.tile(band_table, (1, row_count + 1))[:, :row_count * col_count]  14.2 us
    while x4, local copies, waits for them, and re-layouts  9.72 us
  transfers between devices with their start and end apart: 11, of which 5 were waited for; matrix products, arithmetic and copies ran while one was open for 41% of the time, Pallas kernels for 0%

profile of v1, /device:TPU:3, one launch (start us, length us, event | category | flops | bytes accessed | tf_op | source)
XLA Modules:
  0.0 327.1 jit_solution(7787341624826637662)
XLA Ops:
  8.6 4.2 %collective-permute-start.4 = (bf16[128,2048]{0,1:T(8,128)(2,1)S(1)}, bf16[128,2048]{0,1:T(8,128)(2,1)}, u32[]{:S(2)}, u32[]{:S(2)}) collective-permute-start(bf16[128,2048]{0,1:T(8,128)(2,1)S(1)} %copy.96), channel_id=1, source_target_pairs={{0,4},{4,8},{8,12},{12,16},{16,20},{20,24},{24,28},{28,32},{32,36}... | collective-permute-start | bytes 1572872 | tf_op jit(solution)/shard_map/ppermute | solution.py:20
  12.8 3.5 %collective-permute-start.3 = (bf16[128,2048]{0,1:T(8,128)(2,1)S(1)}, bf16[128,2048]{0,1:T(8,128)(2,1)}, u32[]{:S(2)}, u32[]{:S(2)}) collective-permute-start(bf16[128,2048]{0,1:T(8,128)(2,1)S(1)} %copy.96), channel_id=1, source_target_pairs={{0,8},{4,12},{8,16},{12,20},{16,24},{20,28},{24,32},{28,36},{32,40... | collective-permute-start | bytes 1572872 | tf_op jit(solution)/shard_map/ppermute | solution.py:20
  17.8 1.5 copy.92
  21.2 2.2 collective-permute-start
  27.1 4.4 %tile.8 = bf16[128,129,257]{0,2,1:T(8,128)(2,1)} broadcast(bf16[128,257]{0,1:T(8,128)(2,1)S(1)} %concatenate.19.clone), dimensions={0,2} | broadcast | bytes 8552960 | tf_op jit(solution)/shard_map/tile | solution.py:31
  31.5 13.2 %tile.9 = bf16[128,33153]{0,1:T(8,128)(2,1)} reshape(bf16[128,129,257]{0,2,1:T(8,128)(2,1)} %tile.8) | data formatting | bytes 16974336 | tf_op jit(solution)/shard_map/tile | solution.py:31
  44.7 7.1 %slice.49 = bf16[128,32768]{0,1:T(8,128)(2,1)} slice(bf16[128,33153]{0,1:T(8,128)(2,1)} %tile.9), slice={[0:128], [0:32768]} | slice | bytes 16777216 | tf_op jit(solution)/shard_map/slice | solution.py:31
  51.8 12.3 %copy.95 = bf16[128,128,256]{2,1,0:T(8,128)(2,1)} copy(bf16[128,128,256]{0,2,1:T(8,128)(2,1)} %bitcast.165) | data formatting | bytes 16777216 | tf_op jit(solution)/shard_map/reshape | solution.py:32
  64.6 1.4 pad_maximum_fusion.1
  68.7 4.1 %collective-permute-start.8 = (f32[128,16,128]{0,2,1:T(8,128)S(1)}, f32[128,16,128]{0,2,1:T(8,128)S(1)}, u32[]{:S(2)}, u32[]{:S(2)}) collective-permute-start(f32[128,16,128]{0,2,1:T(8,128)S(1)} %get-tuple-element.138), channel_id=1, source_target_pairs={{8,0},{12,4},{16,8},{20,12},{24,16},{28,20},{32,24},{36,28},{40,32... | collective-permute-start | bytes 3145736 | tf_op jit(solution)/shard_map/ppermute | solution.py:20
  72.8 2.4 collective-permute-start.7
  75.2 1.5 maximum_maximum_fusion
  76.8 2.3 fusion.10
  79.1 16.6 %collective-permute-done.8 = f32[128,16,128]{0,2,1:T(8,128)S(1)} collective-permute-done((f32[128,16,128]{0,2,1:T(8,128)S(1)}, f32[128,16,128]{0,2,1:T(8,128)S(1)}, u32[]{:S(2)}, u32[]{:S(2)}) %collective-permute-start.8) | collective-permute-done | bytes 1048608 | tf_op jit(solution)/shard_map/ppermute | solution.py:20
  95.7 11.4 %collective-permute-done.7 = f32[128,16,128]{0,2,1:T(8,128)S(1)} collective-permute-done((f32[128,16,128]{0,2,1:T(8,128)S(1)}, f32[128,16,128]{0,2,1:T(8,128)S(1)}, u32[]{:S(2)}, u32[]{:S(2)}) %collective-permute-start.7) | collective-permute-done | bytes 1048608 | tf_op jit(solution)/shard_map/ppermute | solution.py:20
  108.3 8.9 %all-reduce.3 = (f32[128]{0:T(128)S(1)}, f32[128]{0:T(128)S(1)}) all-reduce(f32[128]{0:T(128)S(1)} %get-tuple-element.118, f32[128]{0:T(128)S(1)} %get-tuple-element.117), channel_id=1, replica_groups=mesh['context'=32,'mirror'=2,'tensor'=4] {'tensor'}, use_global_device_ids=true, to_apply=%region_4.5 | all-reduce | flops 256 | bytes 2048 | tf_op jit(solution)/shard_map/psum | solution.py:74
  117.2 3.4 %fusion.45 = (bf16[128,2048]{0,1:T(8,128)(2,1)}, bf16[128,2048]{0,1:T(8,128)(2,1)}, bf16[128,2048]{0,1:T(8,128)(2,1)}) fusion(bf16[128,2048]{0,1:T(8,128)(2,1)} %copy.91, f32[128]{0:T(128)S(1)} %get-tuple-element.146, f32[128,16,128]{2,1,0:T(8,128)} %copy-done.1, f32[128,16,128]{0,2,1:T(8,128)} %copy-done.2, f32[2048]{0:T(1024)S(1)} %copy-done.21, ...), kind=kLoop, calls=%fused_computation.55 | loop fusion | flops 3407872 | bytes 4203520 | tf_op jit(solution)/shard_map/convert_element_type | solution.py:135
  120.6 68.2 %while.13 = (s32[]{:T(128)}, f32[4,32,128]{2,1,0:T(8,128)}, bf16[4,128,32,16]{1,3,2,0:T(8,128)(2,1)}, bf16[4,256,32,16]{1,3,2,0:T(8,128)(2,1)}, s32[256]{0:T(256...) while((s32[]{:T(128)}, f32[4,32,128]{2,1,0:T(8,128)}, bf16[4,128,32,16]{1,3,2,0:T(8,128)(2,1)}, ...), condition=%wide.region_14.15_spmd.clone, body=%wide.region_12.14_spmd.clone.sunk | while | flops 35188736 | bytes 32246372 | solution.py:174
  120.7 1.8 convolution_multiply_fusion.2
  122.5 2.4 copy.129
  124.9 2.3 pad.33
  127.2 8.0 %reshape.315 = f32[32,128,257]{2,1,0:T(8,128)} reshape(f32[32,32896]{1,0:T(8,128)} %pad.33) | data formatting | bytes 8421376 | tf_op jit(solution)/shard_map/while/body/eval_jaxpr/reshape | solution.py:165
  135.2 1.7 slice_reduce_fusion.2
  137.7 1.8 convolution_multiply_fusion.2
  139.5 2.4 copy.129
  142.0 2.3 pad.33
  144.3 8.0 %reshape.315 = f32[32,128,257]{2,1,0:T(8,128)} reshape(f32[32,32896]{1,0:T(8,128)} %pad.33) | data formatting | bytes 8421376 | tf_op jit(solution)/shard_map/while/body/eval_jaxpr/reshape | solution.py:165
  152.3 1.7 slice_reduce_fusion.2
  154.8 1.8 convolution_multiply_fusion.2
  156.6 2.4 copy.129
  159.0 2.3 pad.33
  161.4 8.0 %reshape.315 = f32[32,128,257]{2,1,0:T(8,128)} reshape(f32[32,32896]{1,0:T(8,128)} %pad.33) | data formatting | bytes 8421376 | tf_op jit(solution)/shard_map/while/body/eval_jaxpr/reshape | solution.py:165
  169.3 1.7 slice_reduce_fusion.2
  171.8 1.8 convolution_multiply_fusion.2
  173.6 2.4 copy.129
  176.1 2.3 pad.33
  178.4 8.0 %reshape.315 = f32[32,128,257]{2,1,0:T(8,128)} reshape(f32[32,32896]{1,0:T(8,128)} %pad.33) | data formatting | bytes 8421376 | tf_op jit(solution)/shard_map/while/body/eval_jaxpr/reshape | solution.py:165
  186.4 1.7 slice_reduce_fusion.2
  188.8 4.2 %collective-permute-start.9 = (bf16[127,2048]{0,1:T(8,128)(2,1)}, bf16[127,2048]{0,1:T(8,128)(2,1)}, u32[]{:S(2)}, u32[]{:S(2)}) collective-permute-start(bf16[127,2048]{0,1:T(8,128)(2,1)} %bitcast.174), channel_id=1, source_target_pairs={{4,0},{8,4},{12,8},{16,12},{20,16},{24,20},{28,24},{32,28},{36,32}... | collective-permute-start | bytes 1560584 | tf_op jit(solution)/shard_map/ppermute | solution.py:20
  193.2 4.4 %tile.20 = bf16[128,129,257]{0,2,1:T(8,128)(2,1)} broadcast(bf16[128,257]{0,1:T(8,128)(2,1)S(1)} %concatenate.23.clone), dimensions={0,2} | broadcast | bytes 8552960 | tf_op jit(solution)/shard_map/tile | solution.py:31
  197.6 13.2 %tile.21 = bf16[128,33153]{0,1:T(8,128)(2,1)} reshape(bf16[128,129,257]{0,2,1:T(8,128)(2,1)} %tile.20) | data formatting | bytes 16974336 | tf_op jit(solution)/shard_map/tile | solution.py:31
  210.8 7.2 %slice.57 = bf16[128,32768]{0,1:T(8,128)(2,1)} slice(bf16[128,33153]{0,1:T(8,128)(2,1)} %tile.21), slice={[0:128], [0:32768]} | slice | bytes 16777216 | tf_op jit(solution)/shard_map/slice | solution.py:31
  218.0 12.5 %copy.110 = bf16[128,128,256]{2,1,0:T(8,128)(2,1)} copy(bf16[128,128,256]{0,2,1:T(8,128)(2,1)} %bitcast.166) | data formatting | bytes 16777216 | tf_op jit(solution)/shard_map/reshape | solution.py:32
  230.5 1.9 collective-permute-start.2
  232.4 4.6 %collective-permute-start.1 = (bf16[128,2048]{0,1:T(8,128)(2,1)}, bf16[128,2048]{0,1:T(8,128)(2,1)}, u32[]{:S(2)}, u32[]{:S(2)}) collective-permute-start(bf16[128,2048]{0,1:T(8,128)(2,1)} %get-tuple-element.141), channel_id=1, source_target_pairs={{0,8},{4,12},{8,16},{12,20},{16,24},{20,28},{24,32},{28,36},{32,40... | collective-permute-start | bytes 1572872 | tf_op jit(solution)/shard_map/ppermute | solution.py:20
  237.0 2.0 copy.114
  239.0 1.4 maximum_maximum_fusion.1
  240.5 6.7 %fusion.8 = f32[128,16,128]{2,1,0:T(8,128)} fusion(bf16[256,128,16]{0,2,1:T(8,128)(2,1)S(1)} %bitcast.178, bf16[128,128,256]{2,1,0:T(8,128)(2,1)} %copy.110, bf16[128,256]{1,0:T(8,128)(2,1)S(1)} %get-tuple-element.144), kind=kOutput, calls=%fused_computation.11 | convolution fusion | flops 138412032 | bytes 10551296 | tf_op jit(solution)/shard_map/gtu,ugc->tgc/dot_general | solution.py:144
  247.2 18.0 %collective-permute-done.1 = bf16[128,2048]{0,1:T(8,128)(2,1)} collective-permute-done((bf16[128,2048]{0,1:T(8,128)(2,1)}, bf16[128,2048]{0,1:T(8,128)(2,1)}, u32[]{:S(2)}, u32[]{:S(2)}) %collective-permute-start.1) | collective-permute-done | bytes 524320 | tf_op jit(solution)/shard_map/ppermute | solution.py:20
  267.8 2.4 fusion.72
  270.2 6.7 %convolution_bitcast_fusion.1 = f32[384,16,128]{0,2,1:T(8,128)} fusion(bf16[128,16,128]{0,2,1:T(8,128)(2,1)} %bitcast.180, f32[16,384,128]{2,1,0:T(8,128)} %fusion.72, f32[16,384,128]{2,1,0:T(8,128)S(1)} %get-tuple-element.149, f32[16,128]{1,0:T(8,128)S(1)} %log_add_fusion, pred[128,384]{0,1:T(8,128)(4,1)S(1)} %fusion.54), kind=kOutput, calls=%fused_computation.32 | convolution fusion | flops 209979776 | bytes 10018816 | tf_op jit(solution)/shard_map/htu,thd->uhd/dot_general | solution.py:113
  276.9 3.2 fusion.70
  280.2 1.9 collective-permute-start.6
  282.1 1.9 collective-permute-start.5
  285.2 2.0 copy.115
  287.3 2.0 copy.116
  289.3 3.0 convolution_convert_fusion
  292.3 2.0 copy.111
  294.3 6.2 %fusion.44 = bf16[16,128,128]{2,1,0:T(8,128)(2,1)} fusion(bf16[384,16,128]{0,2,1:T(8,128)(2,1)} %bitcast.172, f32[16,384,128]{2,1,0:T(8,128)} %fusion.72, f32[16,384,128]{2,1,0:T(8,128)S(1)} %get-tuple-element.149, f32[16,128]{1,0:T(8,128)S(1)} %log_add_fusion, pred[128,384]{0,1:T(8,128)(4,1)S(1)} %fusion.54), kind=kOutput, calls=%fused_computation.54 | convolution fusion | flops 210241920 | bytes 8445952 | tf_op jit(solution)/shard_map/htu,uhd->thd/dot_general | solution.py:108
  300.5 2.0 copy.112
  302.5 4.7 %collective-permute-done.6 = f32[128,16,128]{0,2,1:T(8,128)} collective-permute-done((f32[128,16,128]{0,2,1:T(8,128)}, f32[128,16,128]{0,2,1:T(8,128)}, u32[]{:S(2)}, u32[]{:S(2)}) %collective-permute-start.6) | collective-permute-done | bytes 1048608 | tf_op jit(solution)/shard_map/ppermute | solution.py:20
  307.3 7.0 %collective-permute-done.5 = f32[128,16,128]{0,2,1:T(8,128)} collective-permute-done((f32[128,16,128]{0,2,1:T(8,128)}, f32[128,16,128]{0,2,1:T(8,128)}, u32[]{:S(2)}, u32[]{:S(2)}) %collective-permute-start.5) | collective-permute-done | bytes 1048608 | tf_op jit(solution)/shard_map/ppermute | solution.py:20
  314.2 2.0 fusion.51
  317.3 3.0 reduce_sum.101
  (106 shorter events, 20.5 us)
Async XLA Ops:
  7.2 16.3 %copy-start.17 = (bf16[128,2048]{1,0:T(8,128)(2,1)S(1)}, bf16[128,2048]{1,0:T(8,128)(2,1)}, u32[]{:S(2)}) copy-start(bf16[128,2048]{1,0:T(8,128)(2,1)} %param.11) | copy-start | bytes 1572868
  7.2 310.1 %all-gather.2.cloned.1.call-start = ((), (), s32[]{:S(2)}) async-start(), calls=%async_computation | async-start | bytes 4259840 | tf_op jit(solution)/shard_map/all_gather | solution.py:12
  8.6 15.9 %copy-start.18 = (bf16[128,2048]{1,0:T(8,128)(2,1)S(1)}, bf16[128,2048]{1,0:T(8,128)(2,1)}, u32[]{:S(2)}) copy-start(bf16[128,2048]{1,0:T(8,128)(2,1)} %param.18) | copy-start | bytes 1572868
  8.6 56.0 %collective-permute-start.4 = (bf16[128,2048]{0,1:T(8,128)(2,1)S(1)}, bf16[128,2048]{0,1:T(8,128)(2,1)}, u32[]{:S(2)}, u32[]{:S(2)}) collective-permute-start(bf16[128,2048]{0,1:T(8,128)(2,1)S(1)} %copy.96), channel_id=1, source_target_pairs={{0,4},{4,8},{8,12},{12,16},{16,20},{20,24},{24,28},{28,32},{32,36}... | collective-permute-start | bytes 1572872 | tf_op jit(solution)/shard_map/ppermute | solution.py:20
  12.8 51.7 %collective-permute-start.3 = (bf16[128,2048]{0,1:T(8,128)(2,1)S(1)}, bf16[128,2048]{0,1:T(8,128)(2,1)}, u32[]{:S(2)}, u32[]{:S(2)}) collective-permute-start(bf16[128,2048]{0,1:T(8,128)(2,1)S(1)} %copy.96), channel_id=1, source_target_pairs={{0,8},{4,12},{8,16},{12,20},{16,24},{20,28},{24,32},{28,36},{32,40... | collective-permute-start | bytes 1572872 | tf_op jit(solution)/shard_map/ppermute | solution.py:20
  17.7 9.1 %copy-start.8 = (bf16[128,2048]{0,1:T(8,128)(2,1)}, bf16[128,2048]{0,1:T(8,128)(2,1)S(1)}, u32[]{:S(2)}) copy-start(bf16[128,2048]{0,1:T(8,128)(2,1)S(1)} %copy.93) | copy-start | bytes 1572868
  17.7 7.7 %copy-start.22 = (s32[4]{0:T(128)S(1)}, s32[4]{0:T(128)}, u32[]{:S(2)}) copy-start(s32[4]{0:T(128)} %param.19) | copy-start | bytes 52
  17.7 8.1 %copy-start.19 = (bf16[128,2048]{1,0:T(8,128)(2,1)S(1)}, bf16[128,2048]{1,0:T(8,128)(2,1)}, u32[]{:S(2)}) copy-start(bf16[128,2048]{1,0:T(8,128)(2,1)} %param.16) | copy-start | bytes 1572868
  19.3 12.3 %copy-start.10 = (bf16[128,2048]{0,1:T(8,128)(2,1)}, bf16[128,2048]{0,1:T(8,128)(2,1)S(1)}, u32[]{:S(2)}) copy-start(bf16[128,2048]{0,1:T(8,128)(2,1)S(1)} %copy.92) | copy-start | bytes 1572868
  19.3 7.6 %copy-start.20 = (bf16[128,128]{1,0:T(8,128)(2,1)S(1)}, bf16[128,128]{1,0:T(8,128)(2,1)}, u32[]{:S(2)}) copy-start(bf16[128,128]{1,0:T(8,128)(2,1)} %param.14) | copy-start | bytes 98308
  19.4 0.8 copy-start.6
  21.2 53.9 %collective-permute-start = (bf16[127,2048]{0,1:T(8,128)(2,1)}, bf16[127,2048]{0,1:T(8,128)(2,1)}, u32[]{:S(2)}, u32[]{:S(2)}) collective-permute-start(bf16[127,2048]{0,1:T(8,128)(2,1)} %slice.48), channel_id=1, source_target_pairs={{0,4},{4,8},{8,12},{12,16},{16,20},{20,24},{24,28},{28,32},{32,36}... | collective-permute-start | bytes 1560584 | tf_op jit(solution)/shard_map/ppermute | solution.py:20
  64.1 1.9 copy-start.16
  66.0 1.5 copy-start.4
  66.0 1.5 copy-start.12
  66.9 9.9 %slice-start = ((s8[8388608]{0:T(1024)(128)(4,1)}), s8[4194304]{0:T(1024)(128)(4,1)S(1)}, s32[]{:S(2)}) async-start(s8[8388608]{0:T(1024)(128)(4,1)} %bitcast.163), calls=%async_computation.1 | async-start | bytes 8388608
  67.6 9.2 %slice-start.1 = ((s8[8388608]{0:T(1024)(128)(4,1)}), s8[4194304]{0:T(1024)(128)(4,1)S(1)}, s32[]{:S(2)}) async-start(s8[8388608]{0:T(1024)(128)(4,1)} %bitcast.163), calls=%async_computation.2 | async-start | bytes 8388608
  68.4 6.8 %copy-start.7 = (bf16[128,2048]{0,1:T(8,128)(2,1)S(1)}, bf16[128,2048]{0,1:T(8,128)(2,1)}, u32[]{:S(2)}) copy-start(bf16[128,2048]{0,1:T(8,128)(2,1)} %copy-done.6) | copy-start | bytes 1572868
  68.7 27.0 %collective-permute-start.8 = (f32[128,16,128]{0,2,1:T(8,128)S(1)}, f32[128,16,128]{0,2,1:T(8,128)S(1)}, u32[]{:S(2)}, u32[]{:S(2)}) collective-permute-start(f32[128,16,128]{0,2,1:T(8,128)S(1)} %get-tuple-element.138), channel_id=1, source_target_pairs={{8,0},{12,4},{16,8},{20,12},{24,16},{28,20},{32,24},{36,28},{40,32... | collective-permute-start | bytes 3145736 | tf_op jit(solution)/shard_map/ppermute | solution.py:20
  72.8 34.3 %collective-permute-start.7 = (f32[128,16,128]{0,2,1:T(8,128)S(1)}, f32[128,16,128]{0,2,1:T(8,128)S(1)}, u32[]{:S(2)}, u32[]{:S(2)}) collective-permute-start(f32[128,16,128]{0,2,1:T(8,128)S(1)} %get-tuple-element.137), channel_id=1, source_target_pairs={{4,0},{8,4},{12,8},{16,12},{20,16},{24,20},{28,24},{32,28},{36,32}... | collective-permute-start | bytes 3145736 | tf_op jit(solution)/shard_map/ppermute | solution.py:20
  76.7 2.3 copy-start
  79.1 28.6 %copy-start.1 = (f32[128,16,128]{2,1,0:T(8,128)}, f32[128,16,128]{2,1,0:T(8,128)S(1)}, u32[]{:S(2)}) copy-start(f32[128,16,128]{2,1,0:T(8,128)S(1)} %fusion.10) | copy-start | bytes 3145732
  79.1 28.2 %copy-start.5 = (bf16[128,2048]{0,1:T(8,128)(2,1)S(1)}, bf16[128,2048]{0,1:T(8,128)(2,1)}, u32[]{:S(2)}) copy-start(bf16[128,2048]{0,1:T(8,128)(2,1)} %copy.91) | copy-start | bytes 1572868
  79.1 28.2 %copy-start.21 = (f32[2048]{0:T(1024)S(1)}, f32[2048]{0:T(1024)}, u32[]{:S(2)}) copy-start(f32[2048]{0:T(1024)} %param.15) | copy-start | bytes 24580
  107.3 1.0 copy-start.2
  188.8 50.2 %collective-permute-start.9 = (bf16[127,2048]{0,1:T(8,128)(2,1)}, bf16[127,2048]{0,1:T(8,128)(2,1)}, u32[]{:S(2)}, u32[]{:S(2)}) collective-permute-start(bf16[127,2048]{0,1:T(8,128)(2,1)} %bitcast.174), channel_id=1, source_target_pairs={{4,0},{8,4},{12,8},{16,12},{20,16},{24,20},{28,24},{32,28},{36,32}... | collective-permute-start | bytes 1560584 | tf_op jit(solution)/shard_map/ppermute | solution.py:20
  230.5 16.7 %collective-permute-start.2 = (bf16[128,2048]{0,1:T(8,128)(2,1)}, bf16[128,2048]{0,1:T(8,128)(2,1)}, u32[]{:S(2)}, u32[]{:S(2)}) collective-permute-start(bf16[128,2048]{0,1:T(8,128)(2,1)} %get-tuple-element.141), channel_id=1, source_target_pairs={{0,4},{4,8},{8,12},{12,16},{16,20},{20,24},{24,28},{28,32},{32,36}... | collective-permute-start | bytes 1572872 | tf_op jit(solution)/shard_map/ppermute | solution.py:20
  232.4 32.8 %collective-permute-start.1 = (bf16[128,2048]{0,1:T(8,128)(2,1)}, bf16[128,2048]{0,1:T(8,128)(2,1)}, u32[]{:S(2)}, u32[]{:S(2)}) collective-permute-start(bf16[128,2048]{0,1:T(8,128)(2,1)} %get-tuple-element.141), channel_id=1, source_target_pairs={{0,8},{4,12},{8,16},{12,20},{16,24},{20,28},{24,32},{28,36},{32,40... | collective-permute-start | bytes 1572872 | tf_op jit(solution)/shard_map/ppermute | solution.py:20
  240.5 24.8 %copy-start.15 = (bf16[128,2048]{0,1:T(8,128)(2,1)S(1)}, bf16[128,2048]{0,1:T(8,128)(2,1)}, u32[]{:S(2)}) copy-start(bf16[128,2048]{0,1:T(8,128)(2,1)} %get-tuple-element.141) | copy-start | bytes 1572868
  247.2 20.6 %copy-start.13 = (bf16[128,2048]{0,1:T(8,128)(2,1)S(1)}, bf16[128,2048]{0,1:T(8,128)(2,1)}, u32[]{:S(2)}) copy-start(bf16[128,2048]{0,1:T(8,128)(2,1)} %copy.126) | copy-start | bytes 1572868
  266.7 1.1 copy-start.3
  276.9 7.1 %copy-start.9 = (bf16[128,2048]{0,1:T(8,128)(2,1)S(1)}, bf16[128,2048]{0,1:T(8,128)(2,1)}, u32[]{:S(2)}) copy-start(bf16[128,2048]{0,1:T(8,128)(2,1)} %copy-done.8) | copy-start | bytes 1572868
  276.9 7.1 %copy-start.11 = (bf16[128,2048]{0,1:T(8,128)(2,1)S(1)}, bf16[128,2048]{0,1:T(8,128)(2,1)}, u32[]{:S(2)}) copy-start(bf16[128,2048]{0,1:T(8,128)(2,1)} %copy-done.10) | copy-start | bytes 1572868
  276.9 7.1 %copy-start.14 = (f32[128,16,128]{2,1,0:T(8,128)S(1)}, f32[128,16,128]{2,1,0:T(8,128)}, u32[]{:S(2)}) copy-start(f32[128,16,128]{2,1,0:T(8,128)} %fusion.8) | copy-start | bytes 3145732
  280.2 27.1 %collective-permute-start.6 = (f32[128,16,128]{0,2,1:T(8,128)}, f32[128,16,128]{0,2,1:T(8,128)}, u32[]{:S(2)}, u32[]{:S(2)}) collective-permute-start(f32[128,16,128]{0,2,1:T(8,128)} %get-tuple-element.136), channel_id=1, source_target_pairs={{8,0},{12,4},{16,8},{20,12},{24,16},{28,20},{32,24},{36,28},{40,32... | collective-permute-start | bytes 3145736 | tf_op jit(solution)/shard_map/ppermute | solution.py:20
  282.1 32.1 %collective-permute-start.5 = (f32[128,16,128]{0,2,1:T(8,128)}, f32[128,16,128]{0,2,1:T(8,128)}, u32[]{:S(2)}, u32[]{:S(2)}) collective-permute-start(f32[128,16,128]{0,2,1:T(8,128)} %get-tuple-element.135), channel_id=1, source_target_pairs={{4,0},{8,4},{12,8},{16,12},{20,16},{24,20},{28,24},{32,28},{36,32}... | collective-permute-start | bytes 3145736 | tf_op jit(solution)/shard_map/ppermute | solution.py:20
Sparse Core Ops, SparseCore 0:
  189.0 80.4 all-gather.1
